TPU v7x, 32 devices: a whole 2x2x4 slice. The times are simulated.
32 devices in a mesh: design: 2 (over x), tile: 8 (over z, y), mode: 2 (over core).
Axes of the slice: x: 2, y: 2, z: 4, core: 2. Of those that a mesh axis runs over, the one named last changes fastest.
Arguments:
- forward: bfloat16 [4, 2, 4096, 4096], P(('design', 'mode'), None, 'tile'), parts along dimension 0, may hold values from -6 to 6
- adjoint_next: bfloat16 [4, 2, 4096, 4096], P(('design', 'mode'), None, 'tile'), parts along dimension 0, may hold values from -6 to 6
- phase: float32 [8192, 4096], P(('design', 'tile'), 'mode'), parts along dimension 0, may hold values from -3.140625 to 3.140625
- blocks: bfloat16 [2, 128, 4, 64, 64], P(None, 'design'), parts along dimension 1, may hold values from -0.25 to 0.25
- offsets: int32 [128, 4], P('design'), parts along dimension 0, may hold values from -2 to 2, as said below
Outputs:
- phase_next: float32 [8192, 4096], P(('design', 'tile'), 'mode'), parts along dimension 0
- forward_next: bfloat16 [4, 2, 4096, 4096], P(('design', 'mode'), None, 'tile'), parts along dimension 0
There are 2 independent parts, one for each index of `design`. A program takes and returns all parts, laid end to end along the dimension named above; each array names one. Nothing has to cross between parts.
Inputs may be any that keep to these rules, and one draw needn't show every extreme that they name: Each row of offsets holds 4 different values, all of -2 to 2 but one; row 0 holds both -2 and 2.
All inputs are finite; a program needn't handle non-finite values.
Results may differ from a plain program's by a relative error of at most 0.02.
Values may be sent and summed in bfloat16 or wider, within the bound.
A program may use at most 256 MiB of HBM per device.

v0:
```python
import jax
import jax.numpy as jnp
from jax import lax
from jax.sharding import PartitionSpec as P

BLK = 64
RADIUS = 2


def dense_operator(blocks_re, blocks_im, shifts, in_blocks):
    out_blocks = shifts.shape[0]
    block_size = blocks_re.shape[-1]
    picks = (
        jnp.arange(out_blocks, dtype=jnp.int32)[:, None, None] + shifts[:, :, None] + RADIUS
        == jnp.arange(in_blocks, dtype=jnp.int32)[None, None, :]
    ).astype(jnp.bfloat16)
    wide_re = jnp.einsum(
        "okb,okij->oibj", picks, blocks_re, preferred_element_type=jnp.float32
    ).astype(jnp.bfloat16)
    wide_im = jnp.einsum(
        "okb,okij->oibj", picks, blocks_im, preferred_element_type=jnp.float32
    ).astype(jnp.bfloat16)
    wide_re = wide_re.reshape(out_blocks * block_size, in_blocks * block_size)
    wide_im = wide_im.reshape(out_blocks * block_size, in_blocks * block_size)
    upper = jnp.stack([wide_re, -wide_im], axis=1)
    lower = jnp.stack([wide_im, wide_re], axis=1)
    return jnp.stack([upper, lower], axis=0)


def column_pass(field_in, operators):
    margin = RADIUS * BLK
    padded = jnp.pad(field_in, ((0, 0), (0, 0), (0, 0), (margin, margin)))
    results = []
    for group, operator in enumerate(operators):
        width_out = operator.shape[1]
        width_in = operator.shape[3]
        window = lax.slice_in_dim(padded, group * width_out, group * width_out + width_in, axis=3)
        results.append(
            jnp.einsum(
                "mprj,qipj->mqri", window, operator, preferred_element_type=jnp.float32
            ).astype(jnp.bfloat16)
        )
    return jnp.concatenate(results, axis=3)


def whole_row_pass(field_in, operators):
    margin = RADIUS * BLK
    padded = jnp.pad(field_in, ((0, 0), (0, 0), (margin, margin), (0, 0)))
    results = []
    for group, operator in enumerate(operators):
        width_out = operator.shape[1]
        width_in = operator.shape[3]
        window = lax.slice_in_dim(padded, group * width_out, group * width_out + width_in, axis=2)
        results.append(
            jnp.einsum(
                "mpjw,qipj->mqiw", window, operator, preferred_element_type=jnp.float32
            ).astype(jnp.bfloat16)
        )
    return jnp.concatenate(results, axis=2)


def row_pass(middle, operators):
    columns = lax.all_to_all(middle, "tile", split_axis=3, concat_axis=2, tiled=True)
    finished = whole_row_pass(columns, operators)
    return lax.all_to_all(finished, "tile", split_axis=2, concat_axis=3, tiled=True)


def body(forward, adjoint_next, phase, blocks, offsets):
    block_total = offsets.shape[0]
    raw_index = jnp.arange(block_total, dtype=jnp.int32)[:, None] + offsets
    inside = (raw_index >= 0) & (raw_index < block_total)
    zero_block = jnp.zeros((), blocks.dtype)
    real_all = jnp.where(inside[:, :, None, None], blocks[0], zero_block)
    imag_all = jnp.where(inside[:, :, None, None], blocks[1], zero_block)
    group_blocks = 8
    operators = []
    for group in range(block_total // group_blocks):
        low = group * group_blocks
        operators.append(
            dense_operator(
                real_all[low : low + group_blocks],
                imag_all[low : low + group_blocks],
                offsets[low : low + group_blocks],
                group_blocks + 2 * RADIUS,
            )
        )
    full_phase = lax.all_gather(phase, "mode", axis=1, tiled=True)
    cos_old = jnp.cos(full_phase)
    sin_old = jnp.sin(full_phase)
    conj_next = jnp.stack([adjoint_next[:, 0], -adjoint_next[:, 1]], axis=1)
    back_middle = column_pass(conj_next, operators)
    conj_here = row_pass(back_middle, operators)
    fwd_real = forward[:, 0].astype(jnp.float32)
    fwd_imag = forward[:, 1].astype(jnp.float32)
    cj_real = conj_here[:, 0].astype(jnp.float32)
    cj_imag = conj_here[:, 1].astype(jnp.float32)
    lit_real = cos_old * fwd_real - sin_old * fwd_imag
    lit_imag = sin_old * fwd_real + cos_old * fwd_imag
    term_real = cj_real * lit_real - cj_imag * lit_imag
    term_imag = cj_real * lit_imag + cj_imag * lit_real
    local_intersection = jnp.stack(
        [jnp.sum(term_real, axis=(1, 2)), jnp.sum(term_imag, axis=(1, 2))], axis=1
    )
    intersections = lax.psum(local_intersection, "tile")
    gradient_part = jnp.sum(
        intersections[:, 0, None, None] * term_imag - intersections[:, 1, None, None] * term_real,
        axis=0,
    )
    scale = 4.0 * full_phase.shape[1] * forward.shape[0] * lax.axis_size("mode")
    half_width = phase.shape[1]
    gradient_full = lax.psum(gradient_part.astype(jnp.bfloat16), "mode").astype(jnp.float32)
    new_full = full_phase - gradient_full / scale
    phase_next = lax.dynamic_slice_in_dim(
        new_full, lax.axis_index("mode") * half_width, half_width, 1
    )
    cos_new = jnp.cos(new_full)
    sin_new = jnp.sin(new_full)
    launched = jnp.stack(
        [cos_new * fwd_real - sin_new * fwd_imag, sin_new * fwd_real + cos_new * fwd_imag], axis=1
    ).astype(jnp.bfloat16)
    forward_middle = column_pass(launched, operators)
    forward_next = row_pass(forward_middle, operators)
    return (phase_next, forward_next)


def solution(mesh):
    placed = (
        P(("design", "mode"), None, "tile", None),
        P(("design", "mode"), None, "tile", None),
        P(("design", "tile"), "mode"),
        P(None, "design", None, None, None),
        P("design", None),
    )
    return jax.shard_map(
        body,
        mesh=mesh,
        in_specs=placed,
        out_specs=(P(("design", "tile"), "mode"), P(("design", "mode"), None, "tile", None)),
        check_vma=False,
    )
```

profile of v0, /device:TPU:0, one launch (start us, length us, event | category | flops | bytes accessed | tf_op | source)
XLA Modules:
  0.0 1371.6 jit_solution(6158530717524008034)
XLA Ops:
  9.0 7.7 fusion.289
  16.8 3.3 convert_bitcast_fusion.14
  21.1 3.2 convert_bitcast_fusion.12
  24.3 3.2 convert_bitcast_fusion.13
  27.6 3.2 convert_bitcast_fusion.10
  30.8 3.3 convert_bitcast_fusion.11
  34.1 3.2 convert_bitcast_fusion.8
  37.3 3.2 convert_bitcast_fusion.9
  40.5 3.2 convert_bitcast_fusion.6
  43.8 3.2 convert_bitcast_fusion.7
  47.0 3.2 convert_bitcast_fusion.4
  50.3 3.2 convert_bitcast_fusion.5
  53.6 3.2 convert_bitcast_fusion.2
  56.8 3.3 convert_bitcast_fusion.3
  60.1 3.2 convert_bitcast_fusion
  63.3 3.2 convert_bitcast_fusion.1
  66.5 3.3 reshape.520
  72.9 5.8 fusion.290
  78.8 3.1 reshape.522
  83.1 3.9 reshape.521
  86.9 3.1 reshape.524
  91.2 4.0 reshape.523
  95.2 3.1 reshape.526
  101.5 3.2 reshape.528
  107.9 3.1 reshape.530
  112.1 3.9 reshape.529
  115.9 3.1 reshape.532
  120.1 3.9 reshape.531
  124.0 3.1 reshape.534
  128.1 4.3 reshape.533
  132.4 4.0 maximum_bitcast_fusion
  136.3 6.3 pad_maximum_fusion
  142.7 2.3 maximum_bitcast_fusion.2
  153.3 2.0 maximum_bitcast_fusion.10
  177.8 32.6 %copy.144 = bf16[1,2,512,4096]{2,1,0,3:T(2,128)(2,1)S(1)} copy(bf16[1,2,512,4096]{2,3,1,0:T(8,128)(2,1)S(1)} %fusion.109) | data formatting | bytes 16777216 | tf_op jit(solution)/shard_map/concatenate | solution.py:43
  210.5 190.2 %all_to_all.72 = bf16[1,2,512,4096]{2,1,0,3:T(2,128)(2,1)} all-to-all(bf16[1,2,512,4096]{2,1,0,3:T(2,128)(2,1)S(1)} %copy.144), channel_id=1, replica_groups=mesh['design'=2,'tile'=8,'mode'=2] {'tile'}, dimensions={3} | all-to-all | bytes 16777216 | tf_op jit(solution)/shard_map/all_to_all | solution.py:63
  400.7 21.1 %copy.145 = bf16[1,2,512,8,512]{4,2,3,1,0:T(8,128)(2,1)} copy(bf16[1,2,512,8,512]{2,1,4,3,0:T(2,128)(2,1)} %bitcast.853) | data formatting | bytes 16777216 | tf_op jit(solution)/shard_map/all_to_all | solution.py:63
  421.9 3.3 fusion.115
  439.6 37.5 %copy.146 = bf16[1,2,4096,512]{3,1,0,2:T(2,128)(2,1)} copy(bf16[1,2,4096,512]{3,2,1,0:T(8,128)(2,1)S(1)} %fusion.133) | data formatting | bytes 16777216 | tf_op jit(solution)/shard_map/concatenate | solution.py:59
  477.0 5.0 all-to-all-start.1
  482.8 22.8 %all-gather.2.cloned.1.call-done = f32[512,4096]{1,0:T(8,128)} async-done(((f32[512,2048]{1,0:T(8,128)}), f32[512,4096]{1,0:T(8,128)}) %all-gather.2.cloned.1.call-update) | async-done | bytes 8388624 | tf_op jit(solution)/shard_map/all_gather | solution.py:87
  505.6 31.9 %fusion.291 = (f32[512,4096]{1,0:T(8,128)}, f32[512,4096]{1,0:T(8,128)}) fusion(f32[512,4096]{1,0:T(8,128)} %all-gather.2.cloned.1.call-done), kind=kLoop, calls=%fused_computation.315 | loop fusion | bytes 25165824 | tf_op jit(solution)/shard_map/sin | solution.py:89
  537.5 126.7 %all-to-all-done.1 = bf16[1,2,4096,512]{3,1,0,2:T(2,128)(2,1)} async-done(((bf16[1,2,4096,512]{3,1,0,2:T(2,128)(2,1)}), bf16[1,2,4096,512]{3,1,0,2:T(2,128)(2,1)}, u32[]{:S(2)}, u32[]{:S(2)}) %all-to-all-start.1) | async-done | bytes 8388640 | tf_op jit(solution)/shard_map/all_to_all | solution.py:65
  664.2 11.4 copy.233
  675.6 13.5 all_to_all.59
  689.1 20.0 %fusion.287 = (f32[]{:T(128)}, f32[512,4096]{1,0:T(8,128)}, f32[]{:T(128)}, f32[512,4096]{1,0:T(8,128)}) fusion(f32[512,4096]{1,0:T(8,128)} %get-tuple-element.16, f32[512,4096]{1,0:T(8,128)} %get-tuple-element.17, bf16[1,2,512,4096]{3,2,1,0:T(8,128)(2,1)} %all_to_all.59, bf16[1,2,512,4096]{3,2,1,0:T(8,128)(2,1)} %param.5), kind=kLoop, calls=%fused_computation.312 | loop fusion | flops 37748736 | bytes 50331656 | tf_op jit(solution)/shard_map/reduce_sum | solution.py:102
  710.5 19.4 %psum.14 = f32[1,2]{1,0:T(1,128)S(1)} all-reduce(f32[1,2]{1,0:T(1,128)S(1)} %pad_maximum_fusion.10), channel_id=1, replica_groups=mesh['design'=2,'tile'=8,'mode'=2] {'tile'}, use_global_device_ids=true, to_apply=%region_2.3 | all-reduce | flops 2 | bytes 16 | tf_op jit(solution)/shard_map/psum | solution.py:104
  730.5 11.2 subtract_convert_fusion
  741.8 25.8 %all-reduce.6.cloned.1.call-done = bf16[512,4096]{1,0:T(8,128)(2,1)} async-done(((bf16[512,4096]{1,0:T(8,128)(2,1)}), bf16[512,4096]{1,0:T(8,128)(2,1)}) %all-reduce.6.cloned.1.call-update) | async-done | bytes 4194320 | tf_op jit(solution)/shard_map/psum | solution.py:111
  767.6 29.0 %fusion.284 = (f32[512,4096]{1,0:T(8,128)S(1)}, f32[512,4096]{1,0:T(8,128)S(1)}) fusion(f32[512,4096]{1,0:T(8,128)} %all-gather.2.cloned.1.call-done, bf16[512,4096]{1,0:T(8,128)(2,1)} %all-reduce.6.cloned.1.call-done), kind=kLoop, calls=%fused_computation.310 | loop fusion | flops 6291456 | bytes 29360128 | tf_op jit(solution)/shard_map/sin | solution.py:117
  796.6 31.5 %fusion.9 = (bf16[1,1,512,4096]{3,2,1,0:T(8,128)(2,1)S(1)}, bf16[1,1,512,4096]{3,2,1,0:T(8,128)(2,1)}) fusion(f32[512,4096]{1,0:T(8,128)S(1)} %get-tuple-element.2, bf16[1,2,512,4096]{3,2,1,0:T(8,128)(2,1)} %param.5, f32[512,4096]{1,0:T(8,128)S(1)} %get-tuple-element.3), kind=kLoop, calls=%fused_computation.58 | loop fusion | flops 20971520 | bytes 33554432 | tf_op jit(solution)/shard_map/stack | solution.py:118
  828.1 6.3 pad_maximum_fusion.1
  834.4 3.8 fusion.139
  851.3 2.0 fusion.181
  853.4 32.6 %copy.148 = bf16[1,2,512,4096]{2,1,0,3:T(2,128)(2,1)S(1)} copy(bf16[1,2,512,4096]{2,3,1,0:T(8,128)(2,1)S(1)} %fusion.181) | data formatting | bytes 16777216 | tf_op jit(solution)/shard_map/concatenate | solution.py:43
  886.0 189.2 %all_to_all.73 = bf16[1,2,512,4096]{2,1,0,3:T(2,128)(2,1)} all-to-all(bf16[1,2,512,4096]{2,1,0,3:T(2,128)(2,1)S(1)} %copy.148), channel_id=1, replica_groups=mesh['design'=2,'tile'=8,'mode'=2] {'tile'}, dimensions={3} | all-to-all | bytes 16777216 | tf_op jit(solution)/shard_map/all_to_all | solution.py:63
  1075.2 21.2 %copy.149 = bf16[1,2,512,8,512]{4,2,3,1,0:T(8,128)(2,1)} copy(bf16[1,2,512,8,512]{2,1,4,3,0:T(2,128)(2,1)} %bitcast.855) | data formatting | bytes 16777216 | tf_op jit(solution)/shard_map/all_to_all | solution.py:63
  1096.4 3.2 fusion.187
  1114.1 37.5 %copy.150 = bf16[1,2,4096,512]{3,1,0,2:T(2,128)(2,1)} copy(bf16[1,2,4096,512]{3,2,1,0:T(8,128)(2,1)S(1)} %fusion.205) | data formatting | bytes 16777216 | tf_op jit(solution)/shard_map/concatenate | solution.py:59
  1151.6 5.2 all-to-all-start.3
  1156.8 4.7 constant_dynamic-slice_fusion
  1161.5 177.9 %all-to-all-done.3 = bf16[1,2,4096,512]{3,1,0,2:T(2,128)(2,1)} async-done(((bf16[1,2,4096,512]{3,1,0,2:T(2,128)(2,1)}), bf16[1,2,4096,512]{3,1,0,2:T(2,128)(2,1)}, u32[]{:S(2)}, u32[]{:S(2)}) %all-to-all-start.3) | async-done | bytes 8388640 | tf_op jit(solution)/shard_map/all_to_all | solution.py:65
  1339.4 11.4 copy.151
  1350.9 13.4 all_to_all.67
  (250 shorter events, 93.3 us)
Async XLA Ops:
  16.8 3.3 copy-start.14
  69.7 9.0 copy-start.12
  81.9 8.2 copy-start.13
  91.2 8.3 copy-start.27
  101.5 4.4 copy-start.28
  104.8 6.3 copy-start.6
  132.4 4.0 copy-start.1
  142.7 2.3 copy-start.11
  142.7 2.3 copy-start.20
  142.7 2.5 copy-start.26
  145.2 19.0 %copy-start.33 = (bf16[1,512,2,768]{3,1,2,0:T(8,128)(2,1)}, bf16[1,512,2,768]{3,1,2,0:T(8,128)(2,1)S(1)}, u32[]{:S(2)}) copy-start(bf16[1,512,2,768]{3,1,2,0:T(8,128)(2,1)S(1)} %get-tuple-element.30) | copy-start | bytes 4718596
  145.3 19.0 %copy-start.37 = (bf16[1,512,2,768]{3,1,2,0:T(8,128)(2,1)}, bf16[1,512,2,768]{3,1,2,0:T(8,128)(2,1)S(1)}, u32[]{:S(2)}) copy-start(bf16[1,512,2,768]{3,1,2,0:T(8,128)(2,1)S(1)} %get-tuple-element.31) | copy-start | bytes 4718596
  145.3 2.5 copy-start.19
  145.3 2.7 copy-start.25
  148.0 18.5 %copy-start.41 = (bf16[1,512,2,768]{3,1,2,0:T(8,128)(2,1)}, bf16[1,512,2,768]{3,1,2,0:T(8,128)(2,1)S(1)}, u32[]{:S(2)}) copy-start(bf16[1,512,2,768]{3,1,2,0:T(8,128)(2,1)S(1)} %get-tuple-element.28) | copy-start | bytes 4718596
  148.0 18.5 %copy-start.45 = (bf16[1,512,2,768]{3,1,2,0:T(8,128)(2,1)}, bf16[1,512,2,768]{3,1,2,0:T(8,128)(2,1)S(1)}, u32[]{:S(2)}) copy-start(bf16[1,512,2,768]{3,1,2,0:T(8,128)(2,1)S(1)} %get-tuple-element.29) | copy-start | bytes 4718596
  148.0 2.5 copy-start.18
  148.0 2.7 copy-start.24
  150.7 17.6 %copy-start.49 = (bf16[1,512,2,768]{3,1,2,0:T(8,128)(2,1)}, bf16[1,512,2,768]{3,1,2,0:T(8,128)(2,1)S(1)}, u32[]{:S(2)}) copy-start(bf16[1,512,2,768]{3,1,2,0:T(8,128)(2,1)S(1)} %get-tuple-element.26) | copy-start | bytes 4718596
  150.7 17.6 %copy-start.53 = (bf16[1,512,2,768]{3,1,2,0:T(8,128)(2,1)}, bf16[1,512,2,768]{3,1,2,0:T(8,128)(2,1)S(1)}, u32[]{:S(2)}) copy-start(bf16[1,512,2,768]{3,1,2,0:T(8,128)(2,1)S(1)} %get-tuple-element.27) | copy-start | bytes 4718596
  150.7 2.5 copy-start.23
  150.8 4.6 copy-start.22
  153.3 16.9 %copy-start.57 = (bf16[1,512,2,768]{3,1,2,0:T(8,128)(2,1)}, bf16[1,512,2,768]{3,1,2,0:T(8,128)(2,1)S(1)}, u32[]{:S(2)}) copy-start(bf16[1,512,2,768]{3,1,2,0:T(8,128)(2,1)S(1)} %get-tuple-element.24) | copy-start | bytes 4718596
  153.3 2.0 copy-start.16
  153.3 4.0 copy-start.21
  153.3 7.2 slice-start
  155.3 3.3 copy-start.15
  155.3 5.8 slice-start.1
  158.6 3.4 copy-start.29
  158.6 3.9 copy-start.30
  162.5 2.2 copy-start.2
  172.1 2.0 copy-start.73
  172.1 2.0 copy-start.77
  400.7 21.1 %copy-start.31 = (bf16[1,512,2,768]{3,1,2,0:T(8,128)(2,1)S(1)}, bf16[1,512,2,768]{3,1,2,0:T(8,128)(2,1)}, u32[]{:S(2)}) copy-start(bf16[1,512,2,768]{3,1,2,0:T(8,128)(2,1)} %get-tuple-element.33) | copy-start | bytes 4718596
  421.9 3.8 copy-start.5
  421.9 4.2 copy-start.34
  421.9 4.6 copy-start.38
  426.5 1.9 copy-start.46
  428.4 1.9 copy-start.54
  477.0 187.2 %all-to-all-start.1 = ((bf16[1,2,4096,512]{3,1,0,2:T(2,128)(2,1)}), bf16[1,2,4096,512]{3,1,0,2:T(2,128)(2,1)}, u32[]{:S(2)}, u32[]{:S(2)}) async-start(bf16[1,2,4096,512]{3,1,0,2:T(2,128)(2,1)} %copy.146), calls=%async_computation.1 | async-start | bytes 16777216 | tf_op jit(solution)/shard_map/all_to_all | solution.py:65
  482.0 23.6 %all-gather.2.cloned.1.call-start = ((), (), s32[]{:S(2)}) async-start(), calls=%async_computation.4 | async-start | bytes 12582912 | tf_op jit(solution)/shard_map/all_gather | solution.py:87
  482.8 284.9 %all-reduce.6.cloned.1.call-start = ((), (), s32[]{:S(2)}) async-start(), calls=%async_computation.5 | async-start | bytes 8388608 | tf_op jit(solution)/shard_map/psum | solution.py:111
  796.6 31.5 %copy-start = (f32[512,4096]{1,0:T(8,128)}, f32[512,4096]{1,0:T(8,128)S(1)}, u32[]{:S(2)}) copy-start(f32[512,4096]{1,0:T(8,128)S(1)} %get-tuple-element.3) | copy-start | bytes 25165828
  834.4 3.8 copy-start.3
  834.4 3.8 copy-start.35
  834.4 4.0 copy-start.39
  838.4 1.9 copy-start.47
  840.3 1.9 copy-start.55
  842.2 1.9 copy-start.63
  844.1 1.9 copy-start.71
  845.9 1.9 copy-start.79
  845.9 3.7 slice-start.2
  847.8 2.7 slice-start.3
  847.8 3.1 copy-start.83
  847.8 3.5 copy-start.87
  1075.2 21.2 %copy-start.32 = (bf16[1,512,2,768]{3,1,2,0:T(8,128)(2,1)S(1)}, bf16[1,512,2,768]{3,1,2,0:T(8,128)(2,1)}, u32[]{:S(2)}) copy-start(bf16[1,512,2,768]{3,1,2,0:T(8,128)(2,1)} %get-tuple-element.33) | copy-start | bytes 4718596
  1096.4 3.8 copy-start.4
  1096.4 4.2 copy-start.36
  1096.4 4.6 copy-start.40
  1101.0 1.9 copy-start.48
  1102.9 1.9 copy-start.56
  1104.8 1.9 copy-start.64
  1106.7 1.9 copy-start.72
  1151.6 187.9 %all-to-all-start.3 = ((bf16[1,2,4096,512]{3,1,0,2:T(2,128)(2,1)}), bf16[1,2,4096,512]{3,1,0,2:T(2,128)(2,1)}, u32[]{:S(2)}, u32[]{:S(2)}) async-start(bf16[1,2,4096,512]{3,1,0,2:T(2,128)(2,1)} %copy.150), calls=%async_computation.3 | async-start | bytes 16777216 | tf_op jit(solution)/shard_map/all_to_all | solution.py:65
  (33 other events, 58.8 us)
Sparse Core Ops, SparseCore 0:
  484.4 21.1 all-gather.1
  741.9 25.6 all-reduce.5
where the time goes:
time: 1380 us; the launch traced here: 1370 us
  blocking collectives  399 us (29%)
  waiting for transfers between devices  354 us (26%)
  local copies, waits for them, and re-layouts  345 us (25%)
  other arithmetic  136 us (10%)
  matrix products  112 us (8%)
  between operations  15.4 us (1%)
    all_to_all x2, blocking collectives, row_pass(): lax.all_to_all(middle, 'tile', split_axis=3, concat_axis=2, tiled=True)  379 us
    all_to_all x2, waiting for transfers between devices, row_pass(): lax.all_to_all(finished, 'tile', split_axis=2, concat_axis=3, tiled=True)  305 us
    concatenate x2, local copies, waits for them, and re-layouts, whole_row_pass(): return jnp.concatenate(results, axis=2)  74.9 us
    concatenate x2, local copies, waits for them, and re-layouts, column_pass(): return jnp.concatenate(results, axis=3)  65.3 us
    all_to_all x4, local copies, waits for them, and re-layouts, row_pass(): lax.all_to_all(finished, 'tile', split_axis=2, concat_axis=3, tiled=True)  49.7 us
    all_to_all x2, local copies, waits for them, and re-layouts, row_pass(): lax.all_to_all(middle, 'tile', split_axis=3, concat_axis=2, tiled=True)  42.3 us
    another operation x2, other arithmetic, body(): jnp.stack([cos_new * fwd_real - sin_new * fwd_imag, sin_new * fwd_real +...  37.8 us
    sin x1, local copies, waits for them, and re-layouts, body(): sin_old = jnp.sin(full_phase)  31.9 us
  transfers between devices with their start and end apart: 4, of which 4 were waited for; matrix products, arithmetic and copies ran while one was open for 3% of the time, Pallas kernels for 0%

commit v1 on v0

--- a/solution.py
+++ b/solution.py
@@ -62,7 +62,10 @@
 def row_pass(middle, operators):
     columns = lax.all_to_all(middle, "tile", split_axis=3, concat_axis=2, tiled=True)
     finished = whole_row_pass(columns, operators)
-    return lax.all_to_all(finished, "tile", split_axis=2, concat_axis=3, tiled=True)
+    return jnp.concatenate(
+        lax.all_to_all(jnp.stack(jnp.split(finished, lax.axis_size("tile"), axis=2)), "tile", 0, 0),
+        axis=3,
+    )
 
 
 def body(forward, adjoint_next, phase, blocks, offsets):

time: 1380 us -> 1330 us (0.964)
  local copies, waits for them, and re-layouts: 345 us -> 272 us
  matrix products: 112 us -> 128 us
    concatenate x2 -> x0, local copies, waits for them, and re-layouts: 74.9 us -> none  [whole_row_pass(): return jnp.concatenate(results, axis=2)]
    all_to_all x4 -> x0, local copies, waits for them, and re-layouts: 49.7 us -> none  [row_pass(): lax.all_to_all(finished, 'tile', split_axis=2, concat_axis=3, tiled=True)]
    sin x1 -> x0, local copies, waits for them, and re-layouts: 31.9 us -> none  [body(): sin_old = jnp.sin(full_phase)]
    cos x0 -> x1, local copies, waits for them, and re-layouts: none -> 31.5 us  [body(): cos_old = jnp.cos(full_phase)]
    reshape x0 -> x2, local copies, waits for them, and re-layouts: none -> 23.7 us  [row_pass(): jnp.concatenate(lax.all_to_all(jnp.stack(jnp.split(finished, lax.axis_siz...]
    unnamed x186 -> x189, local copies, waits for them, and re-layouts: 15.8 us -> 38.5 us
    dot_general x16, matrix products: 31.5 us -> 47.4 us  [whole_row_pass(): jnp.einsum('mpjw,qipj->mqiw', window, operator, preferred_element_type=jn...]
where the time goes in v1:
time: 1330 us; the launch traced here: 1320 us
  blocking collectives  399 us (30%)
  waiting for transfers between devices  354 us (27%)
  local copies, waits for them, and re-layouts  272 us (20%)
  other arithmetic  138 us (10%)
  matrix products  128 us (10%)
  between operations  15 us (1%)
    all_to_all x2, blocking collectives, row_pass(): lax.all_to_all(middle, 'tile', split_axis=3, concat_axis=2, tiled=True)  379 us
    all_to_all x2, waiting for transfers between devices, row_pass(): lax.all_to_all(jnp.stack(jnp.split(finished, lax.axis_size('tile'), axis=...  305 us
    concatenate x2, local copies, waits for them, and re-layouts, column_pass(): return jnp.concatenate(results, axis=3)  65.3 us
    dot_general x16, matrix products, whole_row_pass(): jnp.einsum('mpjw,qipj->mqiw', window, operator, preferred_element_type=jn...  47.4 us
    all_to_all x2, local copies, waits for them, and re-layouts, row_pass(): lax.all_to_all(middle, 'tile', split_axis=3, concat_axis=2, tiled=True)  42.3 us
    unnamed x189, local copies, waits for them, and re-layouts  38.5 us
    another operation x2, other arithmetic, body(): jnp.stack([cos_new * fwd_real - sin_new * fwd_imag, sin_new * fwd_real +...  38 us
    dot_general x16, matrix products, column_pass(): jnp.einsum('mprj,qipj->mqri', window, operator, preferred_element_type=jn...  31.5 us
  transfers between devices with their start and end apart: 4, of which 4 were waited for; matrix products, arithmetic and copies ran while one was open for 3% of the time, Pallas kernels for 0%

profile of v1, /device:TPU:0, one launch (start us, length us, event | category | flops | bytes accessed | tf_op | source)
XLA Modules:
  0.0 1316.5 jit_solution(6090470897520775205)
XLA Ops:
  9.0 7.7 fusion.291
  16.8 3.3 convert_bitcast_fusion.14
  21.1 3.2 convert_bitcast_fusion.12
  24.2 3.2 convert_bitcast_fusion.13
  27.6 3.2 convert_bitcast_fusion.10
  30.8 3.3 convert_bitcast_fusion.11
  34.1 3.2 convert_bitcast_fusion.8
  37.3 3.2 convert_bitcast_fusion.9
  40.5 3.2 convert_bitcast_fusion.6
  43.7 3.2 convert_bitcast_fusion.7
  47.0 3.2 convert_bitcast_fusion.4
  50.3 3.3 convert_bitcast_fusion.5
  53.6 3.2 convert_bitcast_fusion.2
  56.8 3.3 convert_bitcast_fusion.3
  60.1 3.2 convert_bitcast_fusion
  63.3 3.2 convert_bitcast_fusion.1
  66.5 3.3 reshape.552
  72.9 5.8 fusion.292
  78.7 3.1 reshape.554
  83.0 3.9 reshape.553
  86.9 3.1 reshape.556
  91.2 4.0 reshape.555
  95.2 3.1 reshape.558
  101.5 3.2 reshape.560
  107.9 3.1 reshape.562
  112.1 3.9 reshape.561
  116.0 3.1 reshape.564
  120.1 3.9 reshape.563
  124.0 3.1 reshape.566
  128.1 4.3 reshape.565
  132.4 4.0 maximum_bitcast_fusion
  136.4 6.3 pad_maximum_fusion
  177.9 32.6 %copy.145 = bf16[1,2,512,4096]{2,1,0,3:T(2,128)(2,1)S(1)} copy(bf16[1,2,512,4096]{2,3,1,0:T(8,128)(2,1)S(1)} %fusion.109) | data formatting | bytes 16777216 | tf_op jit(solution)/shard_map/concatenate | solution.py:43
  210.5 190.2 %all_to_all.46 = bf16[1,2,512,4096]{2,1,0,3:T(2,128)(2,1)} all-to-all(bf16[1,2,512,4096]{2,1,0,3:T(2,128)(2,1)S(1)} %copy.145), channel_id=1, replica_groups=mesh['design'=2,'tile'=8,'mode'=2] {'tile'}, dimensions={3} | all-to-all | bytes 16777216 | tf_op jit(solution)/shard_map/all_to_all | solution.py:63
  400.8 21.1 %copy.146 = bf16[1,2,512,8,512]{4,2,3,1,0:T(8,128)(2,1)} copy(bf16[1,2,512,8,512]{2,1,4,3,0:T(2,128)(2,1)} %bitcast.837) | data formatting | bytes 16777216 | tf_op jit(solution)/shard_map/all_to_all | solution.py:63
  421.9 4.2 fusion.115
  435.3 2.8 fusion.125
  440.9 2.8 fusion.129
  446.5 5.2 all-to-all-start.1
  452.4 22.8 %all-gather.2.cloned.1.call-done = f32[512,4096]{1,0:T(8,128)} async-done(((f32[512,2048]{1,0:T(8,128)}), f32[512,4096]{1,0:T(8,128)}) %all-gather.2.cloned.1.call-update) | async-done | bytes 8388624 | tf_op jit(solution)/shard_map/all_gather | solution.py:90
  475.2 31.5 %fusion.289 = (f32[512,4096]{1,0:T(8,128)}, f32[512,4096]{1,0:T(8,128)}) fusion(f32[512,4096]{1,0:T(8,128)} %all-gather.2.cloned.1.call-done), kind=kLoop, calls=%fused_computation.310 | loop fusion | bytes 25165824 | tf_op jit(solution)/shard_map/cos | solution.py:91
  506.7 127.1 %all-to-all-done.1 = bf16[8,1,2,512,512]{4,3,2,1,0:T(8,128)(2,1)} async-done(((bf16[8,1,2,512,512]{4,3,2,1,0:T(8,128)(2,1)}), bf16[8,1,2,512,512]{4,3,2,1,0:T(8,128)(2,1)}, u32[]{:S(2)}, u32[]{:S(2)}) %all-to-all-start.1) | async-done | bytes 8388640 | tf_op jit(solution)/shard_map/all_to_all | solution.py:66
  633.8 11.8 copy.147
  645.6 5.9 fusion.290
  651.5 6.4 copy.212
  658.0 6.3 copy.213
  664.3 19.9 %fusion.269 = (f32[]{:T(128)}, f32[]{:T(128)}, f32[512,4096]{1,0:T(8,128)}, f32[512,4096]{1,0:T(8,128)}) fusion(bf16[1,1,512,4096]{3,2,1,0:T(8,128)(2,1)} %copy.213, bf16[1,1,512,4096]{3,2,1,0:T(8,128)(2,1)} %copy.212, f32[512,4096]{1,0:T(8,128)} %get-tuple-element.15, bf16[1,2,512,4096]{3,2,1,0:T(8,128)(2,1)} %param.5, f32[512,4096]{1,0:T(8,128)} %get-tuple-element.14), kind=kLoop, calls=%fused_computation.308 | loop fusion | flops 37748736 | bytes 50331656 | tf_op jit(solution)/shard_map/reduce_sum | solution.py:105
  685.5 19.4 %psum.14 = f32[1,2]{1,0:T(1,128)S(1)} all-reduce(f32[1,2]{1,0:T(1,128)S(1)} %pad_maximum_fusion.10), channel_id=1, replica_groups=mesh['design'=2,'tile'=8,'mode'=2] {'tile'}, use_global_device_ids=true, to_apply=%region_2.3 | all-reduce | flops 2 | bytes 16 | tf_op jit(solution)/shard_map/psum | solution.py:107
  705.6 13.2 %subtract_convert_fusion = bf16[512,4096]{1,0:T(8,128)(2,1)} fusion(f32[]{:T(128)} %bitcast.163, f32[]{:T(128)} %bitcast.162, f32[512,4096]{1,0:T(8,128)} %get-tuple-element.10, bf16[1,1,512,4096]{3,2,1,0:T(8,128)(2,1)} %copy.213, f32[512,4096]{1,0:T(8,128)} %get-tuple-element.11, bf16[1,1,512,4096]{3,2,1,0:T(8,128)(2,1)} %copy.212), kind=kLoop, calls=%fused_computation.47 | loop fusion | flops 25165824 | bytes 29360136 | tf_op jit(solution)/shard_map/convert_element_type | solution.py:114
  718.8 25.9 %all-reduce.6.cloned.1.call-done = bf16[512,4096]{1,0:T(8,128)(2,1)} async-done(((bf16[512,4096]{1,0:T(8,128)(2,1)}), bf16[512,4096]{1,0:T(8,128)(2,1)}) %all-reduce.6.cloned.1.call-update) | async-done | bytes 4194320 | tf_op jit(solution)/shard_map/psum | solution.py:114
  744.6 29.0 %fusion.286 = (f32[512,4096]{1,0:T(8,128)S(1)}, f32[512,4096]{1,0:T(8,128)S(1)}) fusion(f32[512,4096]{1,0:T(8,128)} %all-gather.2.cloned.1.call-done, bf16[512,4096]{1,0:T(8,128)(2,1)} %all-reduce.6.cloned.1.call-done), kind=kLoop, calls=%fused_computation.309 | loop fusion | flops 6291456 | bytes 29360128 | tf_op jit(solution)/shard_map/sin | solution.py:120
  773.6 31.7 %fusion.9 = (bf16[1,1,512,4096]{3,2,1,0:T(8,128)(2,1)S(1)}, bf16[1,1,512,4096]{3,2,1,0:T(8,128)(2,1)}) fusion(f32[512,4096]{1,0:T(8,128)S(1)} %get-tuple-element.8, bf16[1,2,512,4096]{3,2,1,0:T(8,128)(2,1)} %param.5, f32[512,4096]{1,0:T(8,128)S(1)} %get-tuple-element.9), kind=kLoop, calls=%fused_computation.57 | loop fusion | flops 20971520 | bytes 33554432 | tf_op jit(solution)/shard_map/stack | solution.py:121
  805.3 6.3 pad_maximum_fusion.1
  811.6 3.8 fusion.139
  830.6 32.6 %copy.150 = bf16[1,2,512,4096]{2,1,0,3:T(2,128)(2,1)S(1)} copy(bf16[1,2,512,4096]{2,3,1,0:T(8,128)(2,1)S(1)} %fusion.181) | data formatting | bytes 16777216 | tf_op jit(solution)/shard_map/concatenate | solution.py:43
  863.2 189.2 %all_to_all.47 = bf16[1,2,512,4096]{2,1,0,3:T(2,128)(2,1)} all-to-all(bf16[1,2,512,4096]{2,1,0,3:T(2,128)(2,1)S(1)} %copy.150), channel_id=1, replica_groups=mesh['design'=2,'tile'=8,'mode'=2] {'tile'}, dimensions={3} | all-to-all | bytes 16777216 | tf_op jit(solution)/shard_map/all_to_all | solution.py:63
  1052.4 21.2 %copy.151 = bf16[1,2,512,8,512]{4,2,3,1,0:T(8,128)(2,1)} copy(bf16[1,2,512,8,512]{2,1,4,3,0:T(2,128)(2,1)} %bitcast.838) | data formatting | bytes 16777216 | tf_op jit(solution)/shard_map/all_to_all | solution.py:63
  1073.6 4.3 fusion.187
  1092.5 2.8 fusion.201
  1098.1 4.9 all-to-all-start.3
  1103.0 4.7 constant_dynamic-slice_fusion
  1107.7 178.0 %all-to-all-done.3 = bf16[8,1,2,512,512]{4,3,2,1,0:T(8,128)(2,1)} async-done(((bf16[8,1,2,512,512]{4,3,2,1,0:T(8,128)(2,1)}), bf16[8,1,2,512,512]{4,3,2,1,0:T(8,128)(2,1)}, u32[]{:S(2)}, u32[]{:S(2)}) %all-to-all-start.3) | async-done | bytes 8388640 | tf_op jit(solution)/shard_map/all_to_all | solution.py:66
  1285.7 11.9 copy.152
  1297.6 11.9 copy.153
  (250 shorter events, 103.0 us)
Async XLA Ops:
  16.8 3.3 copy-start.14
  69.7 9.0 copy-start.12
  81.8 8.1 copy-start.13
  91.2 8.3 copy-start.27
  101.5 4.4 copy-start.28
  104.8 6.3 copy-start.6
  132.4 4.0 copy-start.1
  145.3 19.1 %copy-start.33 = (bf16[1,512,2,768]{3,1,2,0:T(8,128)(2,1)}, bf16[1,512,2,768]{3,1,2,0:T(8,128)(2,1)S(1)}, u32[]{:S(2)}) copy-start(bf16[1,512,2,768]{3,1,2,0:T(8,128)(2,1)S(1)} %get-tuple-element.34) | copy-start | bytes 4718596
  145.3 19.1 %copy-start.37 = (bf16[1,512,2,768]{3,1,2,0:T(8,128)(2,1)}, bf16[1,512,2,768]{3,1,2,0:T(8,128)(2,1)S(1)}, u32[]{:S(2)}) copy-start(bf16[1,512,2,768]{3,1,2,0:T(8,128)(2,1)S(1)} %get-tuple-element.35) | copy-start | bytes 4718596
  148.0 18.5 %copy-start.41 = (bf16[1,512,2,768]{3,1,2,0:T(8,128)(2,1)}, bf16[1,512,2,768]{3,1,2,0:T(8,128)(2,1)S(1)}, u32[]{:S(2)}) copy-start(bf16[1,512,2,768]{3,1,2,0:T(8,128)(2,1)S(1)} %get-tuple-element.32) | copy-start | bytes 4718596
  148.0 18.5 %copy-start.45 = (bf16[1,512,2,768]{3,1,2,0:T(8,128)(2,1)}, bf16[1,512,2,768]{3,1,2,0:T(8,128)(2,1)S(1)}, u32[]{:S(2)}) copy-start(bf16[1,512,2,768]{3,1,2,0:T(8,128)(2,1)S(1)} %get-tuple-element.33) | copy-start | bytes 4718596
  150.8 17.6 %copy-start.49 = (bf16[1,512,2,768]{3,1,2,0:T(8,128)(2,1)}, bf16[1,512,2,768]{3,1,2,0:T(8,128)(2,1)S(1)}, u32[]{:S(2)}) copy-start(bf16[1,512,2,768]{3,1,2,0:T(8,128)(2,1)S(1)} %get-tuple-element.30) | copy-start | bytes 4718596
  150.8 17.6 %copy-start.53 = (bf16[1,512,2,768]{3,1,2,0:T(8,128)(2,1)}, bf16[1,512,2,768]{3,1,2,0:T(8,128)(2,1)S(1)}, u32[]{:S(2)}) copy-start(bf16[1,512,2,768]{3,1,2,0:T(8,128)(2,1)S(1)} %get-tuple-element.31) | copy-start | bytes 4718596
  150.8 4.5 copy-start.22
  153.3 16.9 %copy-start.57 = (bf16[1,512,2,768]{3,1,2,0:T(8,128)(2,1)}, bf16[1,512,2,768]{3,1,2,0:T(8,128)(2,1)S(1)}, u32[]{:S(2)}) copy-start(bf16[1,512,2,768]{3,1,2,0:T(8,128)(2,1)S(1)} %get-tuple-element.28) | copy-start | bytes 4718596
  153.3 3.9 copy-start.21
  153.3 7.2 slice-start
  155.3 3.3 copy-start.15
  155.3 5.9 slice-start.1
  158.6 3.4 copy-start.29
  158.6 3.9 copy-start.30
  400.8 21.1 %copy-start.31 = (bf16[1,512,2,768]{3,1,2,0:T(8,128)(2,1)S(1)}, bf16[1,512,2,768]{3,1,2,0:T(8,128)(2,1)}, u32[]{:S(2)}) copy-start(bf16[1,512,2,768]{3,1,2,0:T(8,128)(2,1)} %get-tuple-element.37) | copy-start | bytes 4718596
  421.9 4.2 copy-start.5
  421.9 4.2 copy-start.34
  421.9 5.0 copy-start.38
  426.9 2.8 copy-start.42
  426.9 2.8 copy-start.46
  429.7 2.8 copy-start.50
  429.7 2.8 copy-start.54
  432.5 2.8 copy-start.58
  432.5 2.8 copy-start.62
  435.3 2.8 copy-start.66
  435.3 2.8 copy-start.70
  438.1 2.8 copy-start.74
  438.1 2.8 copy-start.78
  440.9 2.8 copy-start.82
  440.9 2.8 copy-start.86
  446.5 187.4 %all-to-all-start.1 = ((bf16[8,1,2,512,512]{4,3,2,1,0:T(8,128)(2,1)}), bf16[8,1,2,512,512]{4,3,2,1,0:T(8,128)(2,1)}, u32[]{:S(2)}, u32[]{:S(2)}) async-start(bf16[8,1,2,512,512]{4,3,2,1,0:T(8,128)(2,1)} %fusion.133), calls=%async_computation.1 | async-start | bytes 16777216 | tf_op jit(solution)/shard_map/all_to_all | solution.py:66
  451.6 23.6 %all-gather.2.cloned.1.call-start = ((), (), s32[]{:S(2)}) async-start(), calls=%async_computation.4 | async-start | bytes 12582912 | tf_op jit(solution)/shard_map/all_gather | solution.py:90
  452.4 292.2 %all-reduce.6.cloned.1.call-start = ((), (), s32[]{:S(2)}) async-start(), calls=%async_computation.5 | async-start | bytes 8388608 | tf_op jit(solution)/shard_map/psum | solution.py:114
  773.6 31.7 %copy-start = (f32[512,4096]{1,0:T(8,128)}, f32[512,4096]{1,0:T(8,128)S(1)}, u32[]{:S(2)}) copy-start(f32[512,4096]{1,0:T(8,128)S(1)} %get-tuple-element.9) | copy-start | bytes 25165828
  811.6 3.8 copy-start.3
  811.6 3.8 copy-start.35
  811.6 4.0 copy-start.39
  823.2 3.7 slice-start.2
  825.0 3.1 copy-start.83
  825.0 3.5 copy-start.87
  1052.4 21.2 %copy-start.32 = (bf16[1,512,2,768]{3,1,2,0:T(8,128)(2,1)S(1)}, bf16[1,512,2,768]{3,1,2,0:T(8,128)(2,1)}, u32[]{:S(2)}) copy-start(bf16[1,512,2,768]{3,1,2,0:T(8,128)(2,1)} %get-tuple-element.37) | copy-start | bytes 4718596
  1073.5 4.3 copy-start.4
  1073.5 4.3 copy-start.36
  1073.5 5.0 copy-start.40
  1078.6 2.8 copy-start.44
  1078.6 2.8 copy-start.48
  1081.3 2.8 copy-start.52
  1081.3 2.8 copy-start.56
  1084.1 2.8 copy-start.60
  1084.1 2.8 copy-start.64
  1086.9 2.8 copy-start.68
  1086.9 2.8 copy-start.72
  1089.7 2.8 copy-start.76
  1089.7 2.8 copy-start.80
  1092.5 2.8 copy-start.84
  1092.5 2.8 copy-start.88
  1098.1 187.6 %all-to-all-start.3 = ((bf16[8,1,2,512,512]{4,3,2,1,0:T(8,128)(2,1)}), bf16[8,1,2,512,512]{4,3,2,1,0:T(8,128)(2,1)}, u32[]{:S(2)}, u32[]{:S(2)}) async-start(bf16[8,1,2,512,512]{4,3,2,1,0:T(8,128)(2,1)} %fusion.205), calls=%async_computation.3 | async-start | bytes 16777216 | tf_op jit(solution)/shard_map/all_to_all | solution.py:66
  (33 other events, 66.4 us)
Sparse Core Ops, SparseCore 0:
  454.0 21.1 all-gather.1
  718.9 25.6 all-reduce.5
